TPU v7x, 256 devices: a whole 4x4x8 slice. The times are simulated.
256 devices in a mesh: src: 16 (over z, core), tgt: 16 (over y, x).
Axes of the slice: x: 4, y: 4, z: 8, core: 2. Of those that a mesh axis runs over, the one named last changes fastest.
Arguments:
- source: float32 [32, 16384], P(None, ('src', 'tgt')), may hold values from -2 to 2
- target: float32 [32, 26624], P(None, ('tgt', 'src')), may hold values from -2 to 2
- target_pot: float32 [26624], P(('tgt', 'src')), may hold values from -1 to 8
- source_logw: float32 [16384], P(('src', 'tgt')), may hold values from -14 to -9
- target_logw: float32 [26624], P(('tgt', 'src')), may hold values from -14 to -9
Outputs:
- f_new: float32 [16384], P(('src', 'tgt'))
- g_new: float32 [26624], P(('tgt', 'src'))
- projection: float32 [32, 16384], P(None, ('src', 'tgt'))
All inputs are finite; a program needn't handle non-finite values.
Results may differ from a plain program's by a relative error of at most 0.0003.
Values sent between devices are 32-bit elements; how exact they have to be, the bound alone decides.
A program may use at most 64 MiB of HBM per device.

v0:
```python
import math
import jax
import jax.numpy as jnp
from jax import lax
from jax.sharding import PartitionSpec as P

EPSILON = 0.05
HIGHEST = lax.Precision.HIGHEST


def cost_scores(row_cells, col_cells, col_sq, col_pot, col_logw):
    cross_term = lax.dot_general(
        row_cells,
        col_cells,
        (((0,), (0,)), ((), ())),
        precision=HIGHEST,
        preferred_element_type=jnp.float32,
    )
    cost_tile = jnp.sum(row_cells * row_cells, 0)[:, None] + col_sq[None, :] - 2.0 * cross_term
    return (col_pot[None, :] - cost_tile) / EPSILON + col_logw[None, :]


def log_sums(row_cells, col_cells, col_pot, col_logw, weighted):
    feat_dim, row_count = row_cells.shape
    row_block = math.gcd(row_count, 512)
    col_sq = jnp.sum(col_cells * col_cells, 0)
    blocks = row_cells.reshape(feat_dim, row_count // row_block, row_block).transpose(1, 0, 2)

    def one_block(cells_block):
        scores = cost_scores(cells_block, col_cells, col_sq, col_pot, col_logw)
        row_top = jnp.max(scores, 1)
        kernel = jnp.exp(scores - row_top[:, None])
        totals = jnp.sum(kernel, 1)
        if weighted:
            moments = lax.dot_general(
                col_cells,
                kernel,
                (((1,), (1,)), ((), ())),
                precision=HIGHEST,
                preferred_element_type=jnp.float32,
            )
            return (row_top, totals, moments)
        return (row_top, totals)

    result = lax.map(one_block, blocks)
    row_top = result[0].reshape(row_count)
    totals = result[1].reshape(row_count)
    if weighted:
        moments = result[2].transpose(1, 0, 2).reshape(feat_dim, row_count)
        return (row_top, totals, moments)
    return (row_top, totals)


def body(source, target, target_pot, source_logw, target_logw):
    src_cells, src_logw = (
        lax.all_gather(source, "tgt", axis=1, tiled=True),
        lax.all_gather(source_logw, "tgt", axis=0, tiled=True),
    )
    tgt_cells, tgt_pot, tgt_logw = (
        lax.all_gather(target, "src", axis=1, tiled=True),
        lax.all_gather(target_pot, "src", axis=0, tiled=True),
        lax.all_gather(target_logw, "src", axis=0, tiled=True),
    )
    row_top, row_totals = log_sums(src_cells, tgt_cells, tgt_pot, tgt_logw, False)
    highest = lax.pmax(row_top, "tgt")
    row_totals = lax.psum(row_totals * jnp.exp(row_top - highest), "tgt")
    row_top = highest
    f_block = -EPSILON * (row_top + jnp.log(row_totals))
    col_top, col_totals = log_sums(tgt_cells, src_cells, f_block, src_logw, False)
    col_highest = lax.pmax(col_top, "src")
    col_totals = lax.psum(col_totals * jnp.exp(col_top - col_highest), "src")
    col_top = col_highest
    g_block = -EPSILON * (col_top + jnp.log(col_totals))
    mine_rows = source.shape[1]
    mine_cols = target.shape[1]
    f_new = lax.dynamic_slice_in_dim(f_block, lax.axis_index("tgt") * mine_rows, mine_rows)
    g_new = lax.dynamic_slice_in_dim(g_block, lax.axis_index("src") * mine_cols, mine_cols)
    proj_top, proj_totals, moments = log_sums(src_cells, tgt_cells, g_block, tgt_logw, True)
    proj_highest = lax.pmax(proj_top, "tgt")
    rescale = jnp.exp(proj_top - proj_highest)
    moments_mine, totals_mine = (
        lax.psum_scatter(moments * rescale[None, :], "tgt", scatter_dimension=1, tiled=True),
        lax.psum_scatter(proj_totals * rescale, "tgt", scatter_dimension=0, tiled=True),
    )
    projection = moments_mine / totals_mine[None, :]
    return (f_new, g_new, projection)


def solution(mesh):
    return jax.shard_map(
        body,
        mesh=mesh,
        in_specs=(
            P(None, ("src", "tgt")),
            P(None, ("tgt", "src")),
            P(("tgt", "src")),
            P(("src", "tgt")),
            P(("tgt", "src")),
        ),
        out_specs=(P(("src", "tgt")), P(("tgt", "src")), P(None, ("src", "tgt"))),
        check_vma=False,
    )
```

profile of v0, /device:TPU:2, one launch (start us, length us, event | category | flops | bytes accessed | tf_op | source)
XLA Modules:
  0.0 446.6 jit_solution(15336664736178391552)
XLA Ops:
  7.3 23.8 %all-gather = f32[16,64,32]{1,2,0:T(8,128)S(1)} all-gather(f32[1,64,32]{1,2,0:T(8,128)} %bitcast.127), channel_id=1, replica_groups=mesh['src'=16,'tgt'=16] {'tgt'}, dimensions={0}, use_global_device_ids=true | all-gather | bytes 139264 | tf_op jit(solution)/shard_map/all_gather | solution.py:56
  32.1 20.9 %all-gather.1 = f32[16,104,32]{1,2,0:T(8,128)S(1)} all-gather(f32[1,104,32]{1,2,0:T(8,128)} %bitcast.128), channel_id=1, replica_groups=mesh['src'=16,'tgt'=16] {'src'}, dimensions={0}, use_global_device_ids=true | all-gather | bytes 226304 | tf_op jit(solution)/shard_map/all_gather | solution.py:60
  54.1 1.6 multiply_reduce_fusion.1
  55.6 1.7 reshape.54
  59.2 45.9 %all-reduce.5 = (f32[1664]{0:T(1024)}, f32[1664]{0:T(1024)}) all-reduce(f32[1664]{0:T(1024)S(1)} %dynamic-update-slice, f32[1664]{0:T(1024)S(1)} %dynamic-update-slice.1), channel_id=1, replica_groups=mesh['src'=16,'tgt'=16] {'src'}, use_global_device_ids=true, to_apply=%add | all-reduce | flops 3328 | bytes 26624
  106.3 15.7 %while.38 = (s32[]{:T(128)}, f32[2,512]{1,0:T(2,128)}, f32[2,512]{1,0:T(2,128)}, f32[1664]{0:T(1024)}, f32[2,32,512]{2,1,0:T(8,128)S(1)}, /*index=5*/f32[1664]{0...) while((s32[]{:T(128)}, f32[2,512]{1,0:T(2,128)}, f32[2,512]{1,0:T(2,128)}, ...), condition=%wide.region_5.6_spmd, body=%wide.region_1.5_spmd.sunk | while | flops 334854656 | bytes 7198333 | solution.py:45
  106.3 4.6 %fusion.41 = (f32[512]{0:T(512)S(1)}, f32[512,1664]{1,0:T(8,128)S(1)}) fusion(f32[1664]{0:T(1024)} %get-tuple-element.476, f32[32,1664]{1,0:T(8,128)} %get-tuple-element.475, f32[2,32,512]{2,1,0:T(8,128)S(1)} %get-tuple-element.473, s32[]{:T(128)S(6)} %copy.48, f32[1664]{0:T(1024)} %get-tuple-element.474, f32[512]{0:T(512)S(1)} %fusion.40, ...), kind=kOutput, calls=%fused_computation.37.clone.1 | convolution fusion | flops 333118976 | bytes 3710468 | tf_op jit(solution)/shard_map/while/body/eval_jaxpr/dot_general | solution.py:12
  114.2 4.6 %fusion.41 = (f32[512]{0:T(512)S(1)}, f32[512,1664]{1,0:T(8,128)S(1)}) fusion(f32[1664]{0:T(1024)} %get-tuple-element.476, f32[32,1664]{1,0:T(8,128)} %get-tuple-element.475, f32[2,32,512]{2,1,0:T(8,128)S(1)} %get-tuple-element.473, s32[]{:T(128)S(6)} %copy.48, f32[1664]{0:T(1024)} %get-tuple-element.474, f32[512]{0:T(512)S(1)} %fusion.40, ...), kind=kOutput, calls=%fused_computation.37.clone.1 | convolution fusion | flops 333118976 | bytes 3710468 | tf_op jit(solution)/shard_map/while/body/eval_jaxpr/dot_general | solution.py:12
  122.6 36.2 %pmax.21 = f32[1024]{0:T(1024)S(1)} all-reduce(f32[1024]{0:T(1024)S(1)} %bitcast.123), channel_id=1, replica_groups=mesh['src'=16,'tgt'=16] {'tgt'}, use_global_device_ids=true, to_apply=%region_6.7 | all-reduce | flops 1024 | bytes 8192 | tf_op jit(solution)/shard_map/pmax | solution.py:65
  159.6 1.3 fusion.21
  162.4 38.6 %all-reduce.4 = (f32[1024]{0:T(1024)S(1)}, f32[1024]{0:T(1024)S(1)}) all-reduce(f32[1024]{0:T(1024)S(1)} %exponential_multiply_fusion, f32[1024]{0:T(1024)S(1)} %dynamic-update-slice.2), channel_id=1, replica_groups=mesh['src'=16,'tgt'=16] {'tgt'}, use_global_device_ids=true, to_apply=%region_7.8 | all-reduce | flops 2048 | bytes 16384 | tf_op jit(solution)/shard_map/psum | solution.py:66
  201.1 54.8 %while.39 = (s32[]{:T(128)}, f32[13,128]{1,0:T(8,128)S(1)}, f32[13,128]{1,0:T(8,128)}, f32[1024]{0:T(1024)S(1)}, f32[13,32,128]{2,0,1:T(8,128)}, /*index=5*/f32[...) while((s32[]{:T(128)}, f32[13,128]{1,0:T(8,128)S(1)}, f32[13,128]{1,0:T(8,128)}, ...), condition=%wide.region_13.14_spmd, body=%wide.region_9.13_spmd.sunk | while | flops 51519104 | bytes 1262201 | solution.py:45
  202.0 1.7 fusion.44
  204.0 1.3 dynamic_update_slice.35
  206.3 1.7 fusion.44
  208.2 1.3 dynamic_update_slice.35
  210.5 1.7 fusion.44
  212.4 1.3 dynamic_update_slice.35
  214.7 1.7 fusion.44
  216.6 1.3 dynamic_update_slice.35
  218.9 1.7 fusion.44
  220.9 1.3 dynamic_update_slice.35
  223.1 1.7 fusion.44
  225.1 1.3 dynamic_update_slice.35
  227.3 1.7 fusion.44
  229.3 1.3 dynamic_update_slice.35
  231.5 1.7 fusion.44
  233.5 1.3 dynamic_update_slice.35
  235.7 1.7 fusion.44
  237.7 1.3 dynamic_update_slice.35
  239.9 1.7 fusion.44
  241.9 1.3 dynamic_update_slice.35
  244.2 1.7 fusion.44
  246.1 1.3 dynamic_update_slice.35
  248.4 1.7 fusion.44
  250.3 1.3 dynamic_update_slice.35
  252.6 1.7 fusion.44
  254.5 1.3 dynamic_update_slice.35
  255.8 24.0 %pmax.22 = f32[1664]{0:T(1024)S(1)} all-reduce(f32[1664]{0:T(1024)S(1)} %bitcast.126), channel_id=1, replica_groups=mesh['src'=16,'tgt'=16] {'src'}, use_global_device_ids=true, to_apply=%region_14.15 | all-reduce | flops 1664 | bytes 13312 | tf_op jit(solution)/shard_map/pmax | solution.py:70
  280.6 24.2 %psum.15 = f32[1664]{0:T(1024)S(1)} all-reduce(f32[1664]{0:T(1024)S(1)} %bitcast_multiply_fusion.2), channel_id=1, replica_groups=mesh['src'=16,'tgt'=16] {'src'}, use_global_device_ids=true, to_apply=%region_15.16 | all-reduce | flops 1664 | bytes 13312 | tf_op jit(solution)/shard_map/psum | solution.py:71
  305.4 21.1 %while.40 = (s32[]{:T(128)}, f32[2,512]{1,0:T(2,128)S(1)}, f32[2,512]{1,0:T(2,128)S(1)}, f32[2,32,512]{2,1,0:T(8,128)}, f32[1664]{0:T(1024)}, /*index=5*/f32[2,3...) while((s32[]{:T(128)}, f32[2,512]{1,0:T(2,128)S(1)}, ...), condition=%wide.region_20.21_spmd, body=%wide.region_16.20_spmd.sunk | while | flops 662862336 | bytes 10886793 | solution.py:45
  305.5 4.6 %fusion.48 = (f32[512]{0:T(512)S(1)}, f32[512,1664]{1,0:T(8,128)S(1)}) fusion(f32[1664]{0:T(1024)} %get-tuple-element.539, f32[32,1664]{1,0:T(8,128)} %get-tuple-element.538, f32[2,32,512]{2,1,0:T(8,128)S(1)} %get-tuple-element.536, s32[]{:T(128)S(6)} %copy.68, f32[1664]{0:T(1024)} %get-tuple-element.537, f32[512]{0:T(512)S(1)} %fusion.47, ...), kind=kOutput, calls=%fused_computation.39.clone.1 | convolution fusion | flops 333118976 | bytes 3710468 | tf_op jit(solution)/shard_map/while/body/eval_jaxpr/dot_general | solution.py:12
  310.8 5.2 %fusion.50 = f32[2,32,512]{2,1,0:T(8,128)} fusion(f32[2,32,512]{2,1,0:T(8,128)} %get-tuple-element.523, s32[]{:T(128)S(6)} %copy.68, f32[32,1664]{1,0:T(8,128)} %get-tuple-element.538, f32[512,1664]{1,0:T(8,128)S(1)} %get-tuple-element.448, f32[512]{0:T(512)S(1)} %get-tuple-element.447), kind=kOutput, calls=%fused_computation.21.clone.1 | convolution fusion | flops 328007680 | bytes 3688452 | tf_op jit(solution)/shard_map/while/body/eval_jaxpr/dot_general | solution.py:35
  316.0 4.6 %fusion.48 = (f32[512]{0:T(512)S(1)}, f32[512,1664]{1,0:T(8,128)S(1)}) fusion(f32[1664]{0:T(1024)} %get-tuple-element.539, f32[32,1664]{1,0:T(8,128)} %get-tuple-element.538, f32[2,32,512]{2,1,0:T(8,128)S(1)} %get-tuple-element.536, s32[]{:T(128)S(6)} %copy.68, f32[1664]{0:T(1024)} %get-tuple-element.537, f32[512]{0:T(512)S(1)} %fusion.47, ...), kind=kOutput, calls=%fused_computation.39.clone.1 | convolution fusion | flops 333118976 | bytes 3710468 | tf_op jit(solution)/shard_map/while/body/eval_jaxpr/dot_general | solution.py:12
  321.3 5.2 %fusion.50 = f32[2,32,512]{2,1,0:T(8,128)} fusion(f32[2,32,512]{2,1,0:T(8,128)} %get-tuple-element.523, s32[]{:T(128)S(6)} %copy.68, f32[32,1664]{1,0:T(8,128)} %get-tuple-element.538, f32[512,1664]{1,0:T(8,128)S(1)} %get-tuple-element.448, f32[512]{0:T(512)S(1)} %get-tuple-element.447), kind=kOutput, calls=%fused_computation.21.clone.1 | convolution fusion | flops 328007680 | bytes 3688452 | tf_op jit(solution)/shard_map/while/body/eval_jaxpr/dot_general | solution.py:35
  327.5 35.5 %pmax.23 = f32[1024]{0:T(1024)S(1)} all-reduce(f32[1024]{0:T(1024)S(1)} %bitcast.121), channel_id=1, replica_groups=mesh['src'=16,'tgt'=16] {'tgt'}, use_global_device_ids=true, to_apply=%region_21.22 | all-reduce | flops 1024 | bytes 8192 | tf_op jit(solution)/shard_map/pmax | solution.py:79
  367.1 37.5 %all-reduce.3 = f32[1024]{0:T(1024)S(1)} all-reduce(f32[1024]{0:T(1024)S(1)} %get-tuple-element.274), channel_id=3, replica_groups=mesh['src'=16,'tgt'=16] {'tgt'}, use_global_device_ids=true, to_apply=%region_23.24.clone | all-reduce | flops 1024 | bytes 8192
  404.7 33.6 %reduce-scatter.4.cloned.1.call-done = f32[64,32]{1,0:T(8,128)} async-done(((f32[1024,32]{1,0:T(8,128)}), f32[64,32]{1,0:T(8,128)}) %reduce-scatter.4.cloned.1.call-update) | async-done | bytes 8208
  (118 shorter events, 37.5 us)
Async XLA Ops:
  7.2 50.1 %copy-start.4 = (u32[256]{0:T(256)S(1)}, u32[256]{0:T(256)}, u32[]{:S(2)}) copy-start(u32[256]{0:T(256)} %constant.89) | copy-start | bytes 3076
  7.2 51.5 %copy-start.2 = (f32[104]{0:T(128)S(1)}, f32[104]{0:T(128)}, u32[]{:S(2)}) copy-start(f32[104]{0:T(128)} %param.13) | copy-start | bytes 1252
  7.2 51.7 %copy-start.3 = (f32[104]{0:T(128)S(1)}, f32[104]{0:T(128)}, u32[]{:S(2)}) copy-start(f32[104]{0:T(128)} %param.15) | copy-start | bytes 1252
  7.2 431.1 %reduce-scatter.4.cloned.1.call-start = ((), (), s32[]{:S(2)}) async-start(), calls=%async_computation.1 | async-start | bytes 557056
  31.3 0.8 copy-start
  255.8 49.6 %copy-start.1 = (f32[1024]{0:T(1024)}, f32[1024]{0:T(1024)S(1)}, u32[]{:S(2)}) copy-start(f32[1024]{0:T(1024)S(1)} %get-tuple-element.549) | copy-start | bytes 12292
Sparse Core Ops, SparseCore 0:
  364.1 74.0 reduce-scatter.3
where the time goes:
time: 448 us; the launch traced here: 447 us
  blocking collectives  287 us (64%)
  matrix products  51 us (11%)
  local copies, waits for them, and re-layouts  49.1 us (11%)
  waiting for transfers between devices  33.6 us (8%)
  between operations  16.1 us (4%)
  other arithmetic  9.89 us (2%)
    unnamed x2, blocking collectives  83.4 us
    dot_general x17, matrix products, cost_scores(): lax.dot_general(row_cells, col_cells, (((0,), (0,)), ((), ())), precision...  40.6 us
    psum x1, blocking collectives, body(): row_totals = lax.psum(row_totals * jnp.exp(row_top - highest), 'tgt')  38.6 us
    pmax x1, blocking collectives, body(): highest = lax.pmax(row_top, 'tgt')  36.2 us
    pmax x1, blocking collectives, body(): proj_highest = lax.pmax(proj_top, 'tgt')  35.5 us
    unnamed x2, waiting for transfers between devices  33.6 us
    psum x1, blocking collectives, body(): col_totals = lax.psum(col_totals * jnp.exp(col_top - col_highest), 'src')  24.2 us
    pmax x1, blocking collectives, body(): col_highest = lax.pmax(col_top, 'src')  24 us
  transfers between devices with their start and end apart: 1, of which 1 were waited for; matrix products, arithmetic and copies ran while one was open for 1% of the time, Pallas kernels for 0%

commit v1 on v0

--- a/solution.py
+++ b/solution.py
@@ -53,7 +53,9 @@
 
 def body(source, target, target_pot, source_logw, target_logw):
     src_cells, src_logw = (
-        lax.all_gather(source, "tgt", axis=1, tiled=True),
+        jnp.concatenate(
+            lax.all_to_all(jnp.stack([source] * lax.axis_size("tgt")), "tgt", 0, 0), axis=1
+        ),
         lax.all_gather(source_logw, "tgt", axis=0, tiled=True),
     )
     tgt_cells, tgt_pot, tgt_logw = (

time: 448 us -> 377 us (0.84)
  local copies, waits for them, and re-layouts: 49.1 us -> 13 us
  blocking collectives: 287 us -> 265 us
  matrix products: 51 us -> 32.4 us
  starting transfers between devices: 0.04 us -> 7.51 us
    all_gather x1 -> x0, blocking collectives: 23.8 us -> none  [body(): lax.all_gather(source, 'tgt', axis=1, tiled=True)]
    dynamic_update_slice x34, local copies, waits for them, and re-layouts: 22.7 us -> 1.3 us  [log_sums(): result = lax.map(one_block, blocks)]
    dot_general x17, matrix products: 40.6 us -> 25.1 us  [cost_scores(): lax.dot_general(row_cells, col_cells, (((0,), (0,)), ((), ())), precision...]
    dynamic_slice x13, local copies, waits for them, and re-layouts: 11.9 us -> 0.29 us  [log_sums(): result = lax.map(one_block, blocks)]
    all_to_all x0 -> x1, starting transfers between devices: none -> 7.48 us  [body(): lax.all_to_all(jnp.stack([source] * lax.axis_size('tgt')), 'tgt', 0, 0)]
  transfers between devices with their start and end apart: 1 -> 2, of which waited for: 1 -> 1; matrix products, arithmetic and copies ran while one was open for 1% -> 2% of each run, Pallas kernels for 0% -> 0%
where the time goes in v1:
time: 377 us; the launch traced here: 376 us
  blocking collectives  265 us (70%)
  waiting for transfers between devices  34.2 us (9%)
  matrix products  32.4 us (9%)
  between operations  16.2 us (4%)
  local copies, waits for them, and re-layouts  13 us (3%)
  other arithmetic  7.6 us (2%)
  starting transfers between devices  7.51 us (2%)
    unnamed x2, blocking collectives  83.4 us
    psum x1, blocking collectives, body(): row_totals = lax.psum(row_totals * jnp.exp(row_top - highest), 'tgt')  40.4 us
    pmax x1, blocking collectives, body(): highest = lax.pmax(row_top, 'tgt')  36.3 us
    pmax x1, blocking collectives, body(): proj_highest = lax.pmax(proj_top, 'tgt')  35.5 us
    unnamed x2, waiting for transfers between devices  34.2 us
    dot_general x17, matrix products, cost_scores(): lax.dot_general(row_cells, col_cells, (((0,), (0,)), ((), ())), precision...  25.1 us
    psum x1, blocking collectives, body(): col_totals = lax.psum(col_totals * jnp.exp(col_top - col_highest), 'src')  24.2 us
    pmax x1, blocking collectives, body(): col_highest = lax.pmax(col_top, 'src')  24.1 us
  transfers between devices with their start and end apart: 2, of which 1 were waited for; matrix products, arithmetic and copies ran while one was open for 2% of the time, Pallas kernels for 0%

profile of v1, /device:TPU:2, one launch (start us, length us, event | category | flops | bytes accessed | tf_op | source)
XLA Modules:
  0.0 376.2 jit_solution(175652257653016064)
XLA Ops:
  7.2 0.7 stack.2
  7.9 0.8 reshape.86
  8.7 7.5 %all-to-all-start = ((f32[16,1,2048]{2,1,0:T(1,128)}), f32[16,1,2048]{2,1,0:T(1,128)S(1)}, u32[]{:S(2)}, u32[]{:S(2)}) async-start(f32[16,1,2048]{2,1,0:T(1,128)} %reshape.86), calls=%async_computation | async-start | bytes 262144 | tf_op jit(solution)/shard_map/all_to_all | solution.py:57
  16.3 20.9 %all-gather = f32[16,104,32]{1,2,0:T(8,128)S(1)} all-gather(f32[1,104,32]{1,2,0:T(8,128)} %bitcast.123), channel_id=1, replica_groups=mesh['src'=16,'tgt'=16] {'src'}, dimensions={0}, use_global_device_ids=true | all-gather | bytes 226304 | tf_op jit(solution)/shard_map/all_gather | solution.py:62
  37.2 1.3 dynamic-slice
  39.1 0.9 dynamic-update-slice
  40.0 0.9 dynamic-update-slice.1
  40.8 45.9 %all-reduce.5 = (f32[1664]{0:T(1024)S(1)}, f32[1664]{0:T(1024)S(1)}) all-reduce(f32[1664]{0:T(1024)S(1)} %dynamic-update-slice, f32[1664]{0:T(1024)S(1)} %dynamic-update-slice.1), channel_id=1, replica_groups=mesh['src'=16,'tgt'=16] {'src'}, use_global_device_ids=true, to_apply=%add | all-reduce | flops 3328 | bytes 26624
  87.1 1.4 fusion.21
  89.2 0.9 dynamic-update-slice.2
  90.6 0.9 reduce.1
  92.3 8.9 %while.38 = (s32[]{:T(128)}, f32[2,512]{1,0:T(2,128)S(1)}, f32[2,512]{1,0:T(2,128)S(1)}, f32[1664]{0:T(1024)S(1)}, f32[2,32,512]{2,1,0:T(8,128)S(1)}, /*index=5*...) while((s32[]{:T(128)}, f32[2,512]{1,0:T(2,128)S(1)}, ...), condition=%wide.region_5.6_spmd, body=%wide.region_1.5_spmd.sunk | while | flops 334854656 | bytes 7202941 | solution.py:45
  92.3 3.7 fusion.41
  96.0 0.6 exponential_reduce_fusion.4
  96.7 3.7 fusion.41
  100.5 0.6 exponential_reduce_fusion.4
  101.2 36.3 %pmax.21 = f32[1024]{0:T(1024)S(1)} all-reduce(f32[1024]{0:T(1024)S(1)} %bitcast.119), channel_id=1, replica_groups=mesh['src'=16,'tgt'=16] {'tgt'}, use_global_device_ids=true, to_apply=%region_6.7 | all-reduce | flops 1024 | bytes 8192 | tf_op jit(solution)/shard_map/pmax | solution.py:67
  137.5 40.4 %all-reduce.4 = (f32[1024]{0:T(1024)S(1)}, f32[1024]{0:T(1024)S(1)}) all-reduce(f32[1024]{0:T(1024)S(1)} %exponential_multiply_fusion, f32[1024]{0:T(1024)S(1)} %dynamic-update-slice.2), channel_id=1, replica_groups=mesh['src'=16,'tgt'=16] {'tgt'}, use_global_device_ids=true, to_apply=%region_7.8 | all-reduce | flops 2048 | bytes 16384 | tf_op jit(solution)/shard_map/psum | solution.py:68
  178.0 15.3 %while.39 = (s32[]{:T(128)}, f32[13,128]{1,0:T(8,128)S(1)}, f32[13,128]{1,0:T(8,128)S(1)}, f32[1024]{0:T(1024)S(1)}, f32[13,32,128]{2,0,1:T(8,128)S(1)}, /*index...) while((s32[]{:T(128)}, f32[13,128]{1,0:T(8,128)S(1)}, ...), condition=%wide.region_13.14_spmd, body=%wide.region_9.13_spmd.sunk | while | flops 51519104 | bytes 1262201 | solution.py:45
  178.0 0.8 fusion.44
  179.2 0.8 fusion.44
  180.4 0.8 fusion.44
  181.5 0.8 fusion.44
  182.7 0.8 fusion.44
  183.9 0.8 fusion.44
  185.1 0.8 fusion.44
  186.2 0.8 fusion.44
  187.4 0.8 fusion.44
  188.6 0.8 fusion.44
  189.8 0.8 fusion.44
  191.0 0.8 fusion.44
  192.1 0.8 fusion.44
  193.2 24.1 %pmax.22 = f32[1664]{0:T(1024)S(1)} all-reduce(f32[1664]{0:T(1024)S(1)} %bitcast.122), channel_id=1, replica_groups=mesh['src'=16,'tgt'=16] {'src'}, use_global_device_ids=true, to_apply=%region_14.15 | all-reduce | flops 1664 | bytes 13312 | tf_op jit(solution)/shard_map/pmax | solution.py:72
  217.3 24.2 %psum.15 = f32[1664]{0:T(1024)S(1)} all-reduce(f32[1664]{0:T(1024)S(1)} %bitcast_multiply_fusion.2), channel_id=1, replica_groups=mesh['src'=16,'tgt'=16] {'src'}, use_global_device_ids=true, to_apply=%region_15.16 | all-reduce | flops 1664 | bytes 13312 | tf_op jit(solution)/shard_map/psum | solution.py:73
  241.6 16.2 %while.40 = (s32[]{:T(128)}, f32[2,512]{1,0:T(2,128)S(1)}, f32[2,512]{1,0:T(2,128)S(1)}, f32[2,32,512]{2,1,0:T(8,128)S(1)}, f32[1664]{0:T(1024)S(1)}, /*index=5*...) while((s32[]{:T(128)}, f32[2,512]{1,0:T(2,128)S(1)}, ...), condition=%wide.region_20.21_spmd, body=%wide.region_16.20_spmd.sunk | while | flops 662862336 | bytes 10891401 | solution.py:45
  241.6 3.7 fusion.48
  245.4 0.6 fusion.49
  246.0 3.6 fusion.50
  249.7 3.7 fusion.48
  253.4 0.6 fusion.49
  254.1 3.6 fusion.50
  257.8 35.5 %pmax.23 = f32[1024]{0:T(1024)S(1)} all-reduce(f32[1024]{0:T(1024)S(1)} %bitcast.117), channel_id=1, replica_groups=mesh['src'=16,'tgt'=16] {'tgt'}, use_global_device_ids=true, to_apply=%region_21.22 | all-reduce | flops 1024 | bytes 8192 | tf_op jit(solution)/shard_map/pmax | solution.py:81
  293.3 1.0 copy.28
  295.0 0.6 dynamic_slice.17
  296.2 37.5 %all-reduce.3 = f32[1024]{0:T(1024)S(1)} all-reduce(f32[1024]{0:T(1024)S(1)} %get-tuple-element.274), channel_id=3, replica_groups=mesh['src'=16,'tgt'=16] {'tgt'}, use_global_device_ids=true, to_apply=%region_23.24.clone | all-reduce | flops 1024 | bytes 8192
  333.7 34.2 %reduce-scatter.4.cloned.1.call-done = f32[64,32]{1,0:T(8,128)} async-done(((f32[1024,32]{1,0:T(8,128)}), f32[64,32]{1,0:T(8,128)}) %reduce-scatter.4.cloned.1.call-update) | async-done | bytes 8208
  367.9 0.8 copy.29
  368.7 0.6 broadcast_divide_fusion
  (115 shorter events, 7.4 us)
Async XLA Ops:
  8.7 81.3 %all-to-all-start = ((f32[16,1,2048]{2,1,0:T(1,128)}), f32[16,1,2048]{2,1,0:T(1,128)S(1)}, u32[]{:S(2)}, u32[]{:S(2)}) async-start(f32[16,1,2048]{2,1,0:T(1,128)} %reshape.86), calls=%async_computation | async-start | bytes 262144 | tf_op jit(solution)/shard_map/all_to_all | solution.py:57
  16.2 351.7 %reduce-scatter.4.cloned.1.call-start = ((), (), s32[]{:S(2)}) async-start(), calls=%async_computation.2 | async-start | bytes 557056
Sparse Core Ops, SparseCore 0:
  294.5 73.3 reduce-scatter.3
